TPU v7x, 256 devices: a whole 4x4x8 slice. The times are simulated.
256 devices in a mesh: wide: 32 (over x, y, core), narrow: 8 (over z).
Axes of the slice: x: 4, y: 4, z: 8, core: 2. Of those that a mesh axis runs over, the one named last changes fastest.
Arguments:
- panels: float32 [256, 512, 512], P('wide', 'narrow'), may hold values from -0.6 to 0.6
- factors: float32 [64, 512, 512], P('wide', 'narrow'), may hold values from -2 to 2
- member: int32 [64, 4], replicated, may hold values from 0 to 255, as said below
- target: int32 [64, 10], replicated, may hold values from 0 to 31
- ancestors: float32 [32, 512, 512], P('wide', 'narrow'), may hold values from -6 to 6
Outputs:
- updated: float32 [32, 512, 512], P('wide', 'narrow')
Inputs may be any that keep to these rules, and one draw needn't show every extreme that they name: `member`: the blocks of supernode s are 4 distinct indices in [(s // 2) * 8, (s // 2 + 1) * 8); every block belongs to exactly one supernode.
All inputs are finite; a program needn't handle non-finite values.
Results may differ from a plain program's by a relative error of at most 0.0003.
Values sent between devices are 32-bit elements; how exact they have to be, the bound alone decides.
No kernel may reach another device: no remote copies, remote signals or barrier semaphores. Data moves between devices by JAX's collectives and lax.ppermute only.
A program may use at most 128 MiB of HBM per device.

v0:
```python
import jax
import jax.numpy as jnp
import numpy as np
from jax import lax
from jax.sharding import PartitionSpec as P


def pair_lists(count):
    left_pick = []
    right_pick = []
    for upper in range(count):
        for lower in range(upper + 1):
            left_pick.append(upper)
            right_pick.append(lower)
    return (np.array(left_pick, dtype=np.int32), np.array(right_pick, dtype=np.int32))


def shards(panels, factors, member, target, ancestors):
    highest = lax.Precision.HIGHEST
    sup_count = factors.shape[0]
    blk_count = panels.shape[0]
    tile_count = ancestors.shape[0] * lax.axis_size("wide")
    left_pick, right_pick = pair_lists(member.shape[1])
    owner_index = lax.axis_index("wide")
    own_members = (
        lax.dynamic_slice_in_dim(member, owner_index * sup_count, sup_count, 0)
        - owner_index * blk_count
    )
    own_targets = lax.dynamic_slice_in_dim(target, owner_index * sup_count, sup_count, 0)
    full_factors = lax.all_gather(factors, "narrow", axis=1, tiled=True)
    blocks = panels[own_members]
    scaled = jnp.einsum("skrw,swv->skrv", blocks, full_factors, precision=highest)
    left_rows = scaled[:, left_pick]
    right_rows = lax.all_gather(scaled, "narrow", axis=2, tiled=True)[:, right_pick]
    updates = jnp.einsum("sprv,spmv->sprm", left_rows, right_rows, precision=highest)
    tile_ids = jnp.arange(tile_count, dtype=jnp.int32)
    onehot = (own_targets[:, :, None] == tile_ids[None, None, :]).astype(jnp.float32)
    portion = jnp.einsum("spa,sprw->arw", onehot, updates, precision=highest)
    totals = lax.psum_scatter(portion, "wide", scatter_dimension=0, tiled=True)
    return ancestors - totals


def solution(mesh):
    return jax.shard_map(
        shards,
        mesh=mesh,
        in_specs=(
            P("wide", "narrow", None),
            P("wide", "narrow", None),
            P(),
            P(),
            P("wide", "narrow", None),
        ),
        out_specs=P("wide", "narrow", None),
        check_vma=False,
    )
```

profile of v0, /device:TPU:2, one launch (start us, length us, event | category | flops | bytes accessed | tf_op | source)
XLA Modules:
  0.0 293.5 jit_solution(6393277430765025806)
XLA Ops:
  6.5 0.7 all-gather.3.cloned.1.call-update
  7.3 0.0 all-gather.5.cloned.1.call-start
  7.3 0.8 compare_select_fusion
  8.1 0.1 copy.15
  8.2 0.1 reshape.3
  8.3 0.0 copy-done
  8.3 0.6 gather_fusion
  8.9 44.1 %all-gather.3.cloned.1.call-done = f32[2,512,512]{2,1,0:T(8,128)} async-done(((f32[2,64,512]{2,1,0:T(8,128)}), f32[2,512,512]{2,1,0:T(8,128)}) %all-gather.3.cloned.1.call-update) | async-done | bytes 2097168 | tf_op jit(solution)/shard_map/all_gather | solution.py:30
  53.0 4.5 %fusion.8 = f32[2,4,64,512]{3,2,1,0:T(8,128)} fusion(f32[2,4,64,512]{3,2,1,0:T(8,128)S(1)} %bitcast.21, f32[2,512,512]{2,1,0:T(8,128)} %all-gather.3.cloned.1.call-done), kind=kOutput, calls=%fused_computation.9 | convolution fusion | flops 1610612736 | bytes 4194304 | tf_op jit(solution)/shard_map/skrw,swv->skrv/dot_general | solution.py:32
  57.5 0.0 all-gather.5.cloned.1.call-update
  57.6 0.0 reduce-scatter.2.cloned.1.call-start
  57.6 0.0 copy-done.3
  57.6 0.1 constant_dynamic-slice_fusion
  57.7 0.1 copy.14
  57.8 0.9 copy-done.1
  58.8 2.2 gather_fusion.1
  60.9 89.4 %all-gather.5.cloned.1.call-done = f32[2,4,512,512]{3,2,1,0:T(8,128)} async-done(((f32[2,4,64,512]{3,2,1,0:T(8,128)}), f32[2,4,512,512]{3,2,1,0:T(8,128)}) %all-gather.5.cloned.1.call-update) | async-done | bytes 8388624 | tf_op jit(solution)/shard_map/all_gather | solution.py:34
  150.3 12.6 %gather_fusion.2 = f32[10,2,512,512]{3,2,1,0:T(8,128)} fusion(f32[2,4,512,512]{3,2,1,0:T(8,128)} %all-gather.5.cloned.1.call-done, s32[1024]{0:T(1024)S(1)} %pad_clamp_fusion), kind=kCustom, calls=%fused_computation.2 | custom fusion | bytes 41943080 | tf_op jit(solution)/shard_map/gather | solution.py:34
  162.9 25.8 %fusion = f32[2,10,64,512]{3,2,1,0:T(8,128)S(1)} fusion(f32[10,2,512,512]{3,2,1,0:T(8,128)} %gather_fusion.2, f32[10,2,64,512]{3,2,1,0:T(8,128)} %gather_fusion.1), kind=kOutput, calls=%fused_computation.3 | convolution fusion | flops 4026531840 | bytes 26214400 | tf_op jit(solution)/shard_map/sprv,spmv->sprm/dot_general | solution.py:35
  188.7 3.9 %fusion.5 = f32[32,64,512]{2,0,1:T(8,128)S(1)} fusion(f32[2,10,64,512]{3,2,1,0:T(8,128)S(1)} %fusion, s32[2,10]{1,0:T(2,128)S(1)} %copy.14), kind=kOutput, calls=%fused_computation.8 | convolution fusion | flops 251658880 | bytes 6815824 | tf_op jit(solution)/shard_map/spa,sprw->arw/dot_general | solution.py:38
  192.6 4.4 %copy.16 = f32[32,64,512]{2,1,0:T(8,128)} copy(f32[32,64,512]{2,0,1:T(8,128)S(1)} %fusion.5) | data formatting | bytes 8388608 | tf_op jit(solution)/shard_map/spa,sprw->arw/dot_general | solution.py:38
  197.0 0.0 reduce-scatter.2.cloned.1.call-update
  197.0 88.4 %reduce-scatter.2.cloned.1.call-done = f32[1,64,512]{2,1,0:T(8,128)} async-done(((f32[32,64,512]{2,1,0:T(8,128)}), f32[1,64,512]{2,1,0:T(8,128)}) %reduce-scatter.2.cloned.1.call-update) | async-done | bytes 131088 | tf_op jit(solution)/shard_map/reduce_scatter | solution.py:39
  285.4 1.6 sub.11
  (13 shorter events, 0.0 us)
Async XLA Ops:
  6.5 1.7 copy-start
  6.5 46.4 %all-gather.3.cloned.1.call-start = ((), (), s32[]{:S(2)}) async-start(), calls=%async_computation.1 | async-start | bytes 2359296 | tf_op jit(solution)/shard_map/all_gather | solution.py:30
  7.3 143.1 %all-gather.5.cloned.1.call-start = ((), (), s32[]{:S(2)}) async-start(), calls=%async_computation.2 | async-start | bytes 9437184 | tf_op jit(solution)/shard_map/all_gather | solution.py:34
  53.0 4.6 %copy-start.3 = (s32[64,10]{0,1:T(8,128)S(1)}, s32[64,10]{0,1:T(8,128)}, u32[]{:S(2)}) copy-start(s32[64,10]{0,1:T(8,128)} %param.12) | copy-start | bytes 7684
  53.0 4.8 %copy-start.5 = (s32[10]{0:T(128)S(1)}, s32[10]{0:T(128)}, u32[]{:S(2)}) copy-start(s32[10]{0:T(128)} %constant.33) | copy-start | bytes 124
  53.0 4.8 %copy-start.4 = (s32[10]{0:T(128)S(1)}, s32[10]{0:T(128)}, u32[]{:S(2)}) copy-start(s32[10]{0:T(128)} %constant.32) | copy-start | bytes 124
  57.5 1.2 copy-start.1
  57.6 227.9 %reduce-scatter.2.cloned.1.call-start = ((), (), s32[]{:S(2)}) async-start(), calls=%async_computation.3 | async-start | bytes 4325376 | tf_op jit(solution)/shard_map/reduce_scatter | solution.py:39
  197.0 88.4 %copy-start.2 = (f32[1,64,512]{2,1,0:T(8,128)S(1)}, f32[1,64,512]{2,1,0:T(8,128)}, u32[]{:S(2)}) copy-start(f32[1,64,512]{2,1,0:T(8,128)} %param.13) | copy-start | bytes 393220
Sparse Core Ops, SparseCore 0:
  9.1 43.8 all-gather.2
  57.7 92.6 all-gather.4
  197.1 88.2 reduce-scatter.1
where the time goes:
time: 294 us
  waiting for transfers between devices  223 us (76%)
  matrix products  34.2 us (12%)
  local copies, waits for them, and re-layouts  21.1 us (7%)
  between operations  13.2 us (4%)
    all_gather x1, waiting for transfers between devices, shards(): lax.all_gather(scaled, 'narrow', axis=2, tiled=True)[:, right_pick]  89.4 us
    reduce_scatter x1, waiting for transfers between devices, shards(): totals = lax.psum_scatter(portion, 'wide', scatter_dimension=0, tiled=True)  88.4 us
    all_gather x1, waiting for transfers between devices, shards(): full_factors = lax.all_gather(factors, 'narrow', axis=1, tiled=True)  44.1 us
    dot_general x1, matrix products, shards(): jnp.einsum('sprv,spmv->sprm', left_rows, right_rows, precision=highest)  25.8 us
    gather x1, local copies, waits for them, and re-layouts, shards(): lax.all_gather(scaled, 'narrow', axis=2, tiled=True)[:, right_pick]  12.6 us
  transfers between devices with their start and end apart: 3, of which 3 were waited for; matrix products, arithmetic and copies ran while one was open for 1% of the time, Pallas kernels for 0%

commit v1 on v0

--- a/solution.py
+++ b/solution.py
@@ -27,9 +27,38 @@
         - owner_index * blk_count
     )
     own_targets = lax.dynamic_slice_in_dim(target, owner_index * sup_count, sup_count, 0)
-    full_factors = lax.all_gather(factors, "narrow", axis=1, tiled=True)
     blocks = panels[own_members]
-    scaled = jnp.einsum("skrw,swv->skrv", blocks, full_factors, precision=highest)
+    peers, index, span = (lax.axis_size("narrow"), lax.axis_index("narrow"), factors.shape[1])
+    right = [(i, (i + 1) % peers) for i in range(peers)]
+    left = [(i, (i - 1) % peers) for i in range(peers)]
+    half = peers // 2
+    from_left = from_right = factors
+    scaled = jnp.einsum(
+        "skrw,swv->skrv",
+        lax.dynamic_slice_in_dim(blocks, index * span, factors.shape[1], axis=3),
+        factors,
+        precision=highest,
+    )
+    for step in range(1, half + 1):
+        from_left = lax.ppermute(from_left, "narrow", right)
+        if step < peers - half:
+            from_right = lax.ppermute(from_right, "narrow", left)
+            scaled = scaled + jnp.einsum(
+                "skrw,swv->skrv",
+                lax.dynamic_slice_in_dim(
+                    blocks, (index + step) % peers * span, from_right.shape[1], axis=3
+                ),
+                from_right,
+                precision=highest,
+            )
+        scaled = scaled + jnp.einsum(
+            "skrw,swv->skrv",
+            lax.dynamic_slice_in_dim(
+                blocks, (index - step) % peers * span, from_left.shape[1], axis=3
+            ),
+            from_left,
+            precision=highest,
+        )
     left_rows = scaled[:, left_pick]
     right_rows = lax.all_gather(scaled, "narrow", axis=2, tiled=True)[:, right_pick]
     updates = jnp.einsum("sprv,spmv->sprm", left_rows, right_rows, precision=highest)

time: 294 us -> 282 us (0.959)
  waiting for transfers between devices: 223 us -> 192 us
  starting transfers between devices: 0.08 us -> 12.5 us
  matrix products: 34.2 us -> 39.9 us
    all_gather x1 -> x0, waiting for transfers between devices: 44.1 us -> none  [shards(): full_factors = lax.all_gather(factors, 'narrow', axis=1, tiled=True)]
    ppermute x0 -> x7, waiting for transfers between devices: none -> 15.9 us  [the longest x4 15.9 us: shards(): from_left = lax.ppermute(from_left, 'narrow', right)]
    ppermute x0 -> x7, starting transfers between devices: none -> 12.4 us  [the longest x3 12.4 us: shards(): from_right = lax.ppermute(from_right, 'narrow', left)]
    dot_general x1 -> x8, matrix products: 4.54 us -> 10.2 us  [the longest x4 5.1 us: shards(): jnp.einsum('skrw,swv->skrv', lax.dynamic_slice_in_dim(blocks, (index - st...]
  transfers between devices with their start and end apart: 3 -> 9, of which waited for: 3 -> 6; matrix products, arithmetic and copies ran while one was open for 1% -> 5% of each run, Pallas kernels for 0% -> 0%
where the time goes in v1:
time: 282 us
  waiting for transfers between devices  192 us (68%)
  matrix products  39.9 us (14%)
  local copies, waits for them, and re-layouts  21.4 us (8%)
  between operations  13.6 us (5%)
  starting transfers between devices  12.5 us (4%)
    reduce_scatter x1, waiting for transfers between devices, shards(): totals = lax.psum_scatter(portion, 'wide', scatter_dimension=0, tiled=True)  88.4 us
    all_gather x1, waiting for transfers between devices, shards(): lax.all_gather(scaled, 'narrow', axis=2, tiled=True)[:, right_pick]  88.1 us
    dot_general x1, matrix products, shards(): jnp.einsum('sprv,spmv->sprm', left_rows, right_rows, precision=highest)  25.8 us
    ppermute x4, waiting for transfers between devices, shards(): from_left = lax.ppermute(from_left, 'narrow', right)  15.9 us
    gather x1, local copies, waits for them, and re-layouts, shards(): lax.all_gather(scaled, 'narrow', axis=2, tiled=True)[:, right_pick]  12.6 us
    ppermute x3, starting transfers between devices, shards(): from_right = lax.ppermute(from_right, 'narrow', left)  12.4 us
  transfers between devices with their start and end apart: 9, of which 6 were waited for; matrix products, arithmetic and copies ran while one was open for 5% of the time, Pallas kernels for 0%

profile of v1, /device:TPU:2, one launch (start us, length us, event | category | flops | bytes accessed | tf_op | source)
XLA Modules:
  0.0 282.2 jit_solution(4167703075052496583)
XLA Ops:
  6.5 5.9 %collective-permute-start = (f32[2,64,512]{2,1,0:T(8,128)}, f32[2,64,512]{2,1,0:T(8,128)S(1)}, u32[]{:S(2)}, u32[]{:S(2)}) collective-permute-start(f32[2,64,512]{2,1,0:T(8,128)} %param.10), channel_id=1, source_target_pairs={{0,7},{1,0},{2,1},{3,2},{4,3},{5,4},{6,5},{7,6},{8,15},{9,8},{10,9... | collective-permute-start | bytes 786440 | tf_op jit(solution)/shard_map/ppermute | solution.py:45
  12.4 0.8 compare_select_fusion
  14.1 2.0 fusion.19
  16.0 5.5 %collective-permute-done.1 = f32[2,64,512]{2,1,0:T(8,128)S(1)} collective-permute-done((f32[2,64,512]{2,1,0:T(8,128)}, f32[2,64,512]{2,1,0:T(8,128)S(1)}, u32[]{:S(2)}, u32[]{:S(2)}) %collective-permute-start.1) | collective-permute-done | bytes 262176 | tf_op jit(solution)/shard_map/ppermute | solution.py:43
  21.6 3.2 %collective-permute-start.2 = (f32[2,64,512]{2,1,0:T(8,128)S(1)}, f32[2,64,512]{2,1,0:T(8,128)S(1)}, u32[]{:S(2)}, u32[]{:S(2)}) collective-permute-start(f32[2,64,512]{2,1,0:T(8,128)S(1)} %collective-permute-done), channel_id=1, source_target_pairs={{0,7},{1,0},{2,1},{3,2},{4,3},{5,4},{6,5},{7,6},{8,15},{9,8},{10,9... | collective-permute-start | bytes 786440 | tf_op jit(solution)/shard_map/ppermute | solution.py:45
  24.8 1.0 convolution_add_fusion.4
  25.9 1.0 convolution_add_fusion.3
  26.9 2.8 collective-permute-done.3
  29.7 1.0 fusion.14
  30.8 3.3 %collective-permute-start.4 = (f32[2,64,512]{2,1,0:T(8,128)S(1)}, f32[2,64,512]{2,1,0:T(8,128)S(1)}, u32[]{:S(2)}, u32[]{:S(2)}) collective-permute-start(f32[2,64,512]{2,1,0:T(8,128)S(1)} %collective-permute-done.2), channel_id=1, source_target_pairs={{0,7},{1,0},{2,1},{3,2},{4,3},{5,4},{6,5},{7,6},{8,15},{9,8},{10,9... | collective-permute-start | bytes 786440 | tf_op jit(solution)/shard_map/ppermute | solution.py:45
  34.1 1.1 fusion.9
  35.2 2.1 collective-permute-done.5
  37.3 1.0 fusion.11
  38.3 1.1 fusion.8
  39.4 5.5 %collective-permute-done.6 = f32[2,64,512]{2,1,0:T(8,128)S(1)} collective-permute-done((f32[2,64,512]{2,1,0:T(8,128)S(1)}, f32[2,64,512]{2,1,0:T(8,128)S(1)}, u32[]{:S(2)}, u32[]{:S(2)}) %collective-permute-start.6) | collective-permute-done | bytes 262176 | tf_op jit(solution)/shard_map/ppermute | solution.py:43
  44.9 2.0 convolution_add_fusion
  47.2 3.4 %gather_fusion.1 = f32[10,2,64,512]{3,2,1,0:T(8,128)} fusion(f32[2,4,64,512]{3,2,1,0:T(8,128)} %convolution_add_fusion, s32[1024]{0:T(1024)S(1)} %pad_clamp_fusion.1), kind=kCustom, calls=%fused_computation.1 | custom fusion | bytes 5242920 | tf_op jit(solution)/shard_map/gather | solution.py:62
  50.6 88.1 %all-gather.2.cloned.1.call-done = f32[2,4,512,512]{3,2,1,0:T(8,128)} async-done(((f32[2,4,64,512]{3,2,1,0:T(8,128)}), f32[2,4,512,512]{3,2,1,0:T(8,128)}) %all-gather.2.cloned.1.call-update) | async-done | bytes 8388624 | tf_op jit(solution)/shard_map/all_gather | solution.py:63
  138.7 12.6 %gather_fusion.2 = f32[10,2,512,512]{3,2,1,0:T(8,128)} fusion(f32[2,4,512,512]{3,2,1,0:T(8,128)} %all-gather.2.cloned.1.call-done, s32[1024]{0:T(1024)S(1)} %pad_clamp_fusion), kind=kCustom, calls=%fused_computation.2 | custom fusion | bytes 41943080 | tf_op jit(solution)/shard_map/gather | solution.py:63
  151.3 25.8 %fusion = f32[2,10,64,512]{3,2,1,0:T(8,128)S(1)} fusion(f32[10,2,512,512]{3,2,1,0:T(8,128)} %gather_fusion.2, f32[10,2,64,512]{3,2,1,0:T(8,128)} %gather_fusion.1), kind=kOutput, calls=%fused_computation.3 | convolution fusion | flops 4026531840 | bytes 26214400 | tf_op jit(solution)/shard_map/sprv,spmv->sprm/dot_general | solution.py:64
  177.1 3.9 %fusion.5 = f32[32,64,512]{2,0,1:T(8,128)S(1)} fusion(f32[2,10,64,512]{3,2,1,0:T(8,128)S(1)} %fusion, s32[2,10]{1,0:T(2,128)S(1)} %copy.14), kind=kOutput, calls=%fused_computation.8 | convolution fusion | flops 251658880 | bytes 6815824 | tf_op jit(solution)/shard_map/spa,sprw->arw/dot_general | solution.py:67
  181.0 4.4 %copy.16 = f32[32,64,512]{2,1,0:T(8,128)} copy(f32[32,64,512]{2,0,1:T(8,128)S(1)} %fusion.5) | data formatting | bytes 8388608 | tf_op jit(solution)/shard_map/spa,sprw->arw/dot_general | solution.py:67
  185.4 88.4 %reduce-scatter.2.cloned.1.call-done = f32[1,64,512]{2,1,0:T(8,128)} async-done(((f32[32,64,512]{2,1,0:T(8,128)}), f32[1,64,512]{2,1,0:T(8,128)}) %reduce-scatter.2.cloned.1.call-update) | async-done | bytes 131088 | tf_op jit(solution)/shard_map/reduce_scatter | solution.py:68
  273.8 1.6 sub.27
  (29 shorter events, 1.1 us)
Async XLA Ops:
  6.5 6.9 %copy-start = (f32[8,64,512]{2,1,0:T(8,128)S(1)}, f32[8,64,512]{2,1,0:T(8,128)}, u32[]{:S(2)}) copy-start(f32[8,64,512]{2,1,0:T(8,128)} %param.9) | copy-start | bytes 3145732
  6.5 132.1 %all-gather.2.cloned.1.call-start = ((), (), s32[]{:S(2)}) async-start(), calls=%async_computation.1 | async-start | bytes 9437184 | tf_op jit(solution)/shard_map/all_gather | solution.py:63
  6.5 15.1 %collective-permute-start = (f32[2,64,512]{2,1,0:T(8,128)}, f32[2,64,512]{2,1,0:T(8,128)S(1)}, u32[]{:S(2)}, u32[]{:S(2)}) collective-permute-start(f32[2,64,512]{2,1,0:T(8,128)} %param.10), channel_id=1, source_target_pairs={{0,7},{1,0},{2,1},{3,2},{4,3},{5,4},{6,5},{7,6},{8,15},{9,8},{10,9... | collective-permute-start | bytes 786440 | tf_op jit(solution)/shard_map/ppermute | solution.py:45
  12.4 9.2 %collective-permute-start.1 = (f32[2,64,512]{2,1,0:T(8,128)}, f32[2,64,512]{2,1,0:T(8,128)S(1)}, u32[]{:S(2)}, u32[]{:S(2)}) collective-permute-start(f32[2,64,512]{2,1,0:T(8,128)} %param.10), channel_id=1, source_target_pairs={{0,1},{1,2},{2,3},{3,4},{4,5},{5,6},{6,7},{7,0},{8,9},{9,10},{10,1... | collective-permute-start | bytes 786440 | tf_op jit(solution)/shard_map/ppermute | solution.py:43
  21.6 8.1 %collective-permute-start.3 = (f32[2,64,512]{2,1,0:T(8,128)S(1)}, f32[2,64,512]{2,1,0:T(8,128)S(1)}, u32[]{:S(2)}, u32[]{:S(2)}) collective-permute-start(f32[2,64,512]{2,1,0:T(8,128)S(1)} %collective-permute-done.1), channel_id=1, source_target_pairs={{0,1},{1,2},{2,3},{3,4},{4,5},{5,6},{6,7},{7,0},{8,9},{9,10},{10,1... | collective-permute-start | bytes 786440 | tf_op jit(solution)/shard_map/ppermute | solution.py:43
  21.6 9.2 %collective-permute-start.2 = (f32[2,64,512]{2,1,0:T(8,128)S(1)}, f32[2,64,512]{2,1,0:T(8,128)S(1)}, u32[]{:S(2)}, u32[]{:S(2)}) collective-permute-start(f32[2,64,512]{2,1,0:T(8,128)S(1)} %collective-permute-done), channel_id=1, source_target_pairs={{0,7},{1,0},{2,1},{3,2},{4,3},{5,4},{6,5},{7,6},{8,15},{9,8},{10,9... | collective-permute-start | bytes 786440 | tf_op jit(solution)/shard_map/ppermute | solution.py:45
  29.7 7.6 %collective-permute-start.5 = (f32[2,64,512]{2,1,0:T(8,128)S(1)}, f32[2,64,512]{2,1,0:T(8,128)S(1)}, u32[]{:S(2)}, u32[]{:S(2)}) collective-permute-start(f32[2,64,512]{2,1,0:T(8,128)S(1)} %collective-permute-done.3), channel_id=1, source_target_pairs={{0,1},{1,2},{2,3},{3,4},{4,5},{5,6},{6,7},{7,0},{8,9},{9,10},{10,1... | collective-permute-start | bytes 786440 | tf_op jit(solution)/shard_map/ppermute | solution.py:43
  30.8 7.6 %collective-permute-start.4 = (f32[2,64,512]{2,1,0:T(8,128)S(1)}, f32[2,64,512]{2,1,0:T(8,128)S(1)}, u32[]{:S(2)}, u32[]{:S(2)}) collective-permute-start(f32[2,64,512]{2,1,0:T(8,128)S(1)} %collective-permute-done.2), channel_id=1, source_target_pairs={{0,7},{1,0},{2,1},{3,2},{4,3},{5,4},{6,5},{7,6},{8,15},{9,8},{10,9... | collective-permute-start | bytes 786440 | tf_op jit(solution)/shard_map/ppermute | solution.py:45
  35.1 11.8 %copy-start.2 = (s32[64,10]{0,1:T(8,128)S(1)}, s32[64,10]{0,1:T(8,128)}, u32[]{:S(2)}) copy-start(s32[64,10]{0,1:T(8,128)} %param.12) | copy-start | bytes 7684
  35.1 12.0 %copy-start.4 = (s32[10]{0:T(128)S(1)}, s32[10]{0:T(128)}, u32[]{:S(2)}) copy-start(s32[10]{0:T(128)} %constant.85) | copy-start | bytes 124
  35.2 12.0 %copy-start.3 = (s32[10]{0:T(128)S(1)}, s32[10]{0:T(128)}, u32[]{:S(2)}) copy-start(s32[10]{0:T(128)} %constant.84) | copy-start | bytes 124
  37.3 7.6 %collective-permute-start.6 = (f32[2,64,512]{2,1,0:T(8,128)S(1)}, f32[2,64,512]{2,1,0:T(8,128)S(1)}, u32[]{:S(2)}, u32[]{:S(2)}) collective-permute-start(f32[2,64,512]{2,1,0:T(8,128)S(1)} %collective-permute-done.5), channel_id=1, source_target_pairs={{0,1},{1,2},{2,3},{3,4},{4,5},{5,6},{6,7},{7,0},{8,9},{9,10},{10,1... | collective-permute-start | bytes 786440 | tf_op jit(solution)/shard_map/ppermute | solution.py:43
  46.9 226.9 %reduce-scatter.2.cloned.1.call-start = ((), (), s32[]{:S(2)}) async-start(), calls=%async_computation.2 | async-start | bytes 4325376 | tf_op jit(solution)/shard_map/reduce_scatter | solution.py:68
  185.4 88.4 %copy-start.1 = (f32[1,64,512]{2,1,0:T(8,128)S(1)}, f32[1,64,512]{2,1,0:T(8,128)}, u32[]{:S(2)}) copy-start(f32[1,64,512]{2,1,0:T(8,128)} %param.13) | copy-start | bytes 393220
Sparse Core Ops, SparseCore 0:
  47.0 91.6 all-gather.1
  185.5 88.2 reduce-scatter.1
